TPU v7x, 32 devices: a whole 2x2x4 slice. The times are simulated.
32 devices in a mesh: groups: 2 (over y), emit: 4 (over z), recv: 4 (over x, core).
Axes of the slice: x: 2, y: 2, z: 4, core: 2. Of those that a mesh axis runs over, the one named last changes fastest.
Arguments:
- positions: float32 [3, 8192], P(None, ('groups', 'emit', 'recv')), parts along dimension 1, may hold values from 0 to 1
- angles: float32 [2, 8192], P(None, ('groups', 'emit', 'recv')), parts along dimension 1, may hold values from -3.140625 to 3.140625
- areas: float32 [8192], P(('groups', 'emit', 'recv')), parts along dimension 0, may hold values from 0.00024414062 to 0.00390625
- emissivity: float32 [8192], P(('groups', 'emit', 'recv')), parts along dimension 0, may hold values from 0.1 to 0.9
- emission: float32 [32, 8192], P(None, ('groups', 'emit', 'recv')), parts along dimension 1, may hold values from 0.5 to 2
- radiosity_in: float32 [32, 8192], P(None, ('groups', 'emit', 'recv')), parts along dimension 1, may hold values from 0.2 to 2
- adjoint_in: float32 [32, 8192], P(None, ('groups', 'emit', 'recv')), parts along dimension 1, may hold values from 0 to 1.5
- visibility: int32 [64, 32], P(('groups', 'emit')), parts along dimension 0, may hold values 0 or 1
- inlet_patches: int32 [4096], P('groups'), parts along dimension 0, may hold values from 0 to 4095
- inlet_weights: float32 [32, 4096], P(None, 'groups'), parts along dimension 1, may hold values from 0.5 to 2
Outputs:
- radiosity_out: float32 [32, 8192], P(None, ('groups', 'emit', 'recv')), parts along dimension 1
- adjoint_out: float32 [32, 8192], P(None, ('groups', 'emit', 'recv')), parts along dimension 1
- emissivity_grad: float32 [8192], P(('groups', 'emit', 'recv')), parts along dimension 0
There are 2 independent parts, one for each index of `groups`. A program takes and returns all parts, laid end to end along the dimension named above; each array names one. Nothing has to cross between parts.
Inputs may be any that keep to these rules, and one draw needn't show every extreme that they name: `inlet_patches`: an inlet patch may be listed more than once.
All inputs are finite; a program needn't handle non-finite values. No bound on the sum of `visibility` on one device may be relied on, other than what follows from the above.
Results may differ from a plain program's by a relative error of at most 0.0003.
Values may be sent and summed in bfloat16 or wider, within the bound.
No kernel may reach another device: no remote copies, remote signals or barrier semaphores. Data moves between devices by JAX's collectives and lax.ppermute only.
A program may use at most 64 MiB of HBM per device.

v0:
```python
import math
import jax
import jax.numpy as jnp
from jax import lax
from jax.sharding import PartitionSpec as P

BLK = 128


def patch_geometry(positions, angles, areas):
    polar = angles[0]
    azimuth = angles[1]
    normal = jnp.stack(
        [jnp.sin(polar) * jnp.cos(azimuth), jnp.sin(polar) * jnp.sin(azimuth), jnp.cos(polar)]
    )
    return jnp.concatenate([positions, normal, areas[None, :]], axis=0)


def view_tile(row_geom, col_geom, block_mask):
    delta_x = col_geom[0][None, :] - row_geom[0][:, None]
    delta_y = col_geom[1][None, :] - row_geom[1][:, None]
    delta_z = col_geom[2][None, :] - row_geom[2][:, None]
    dist_sq = delta_x * delta_x + delta_y * delta_y + delta_z * delta_z
    cos_emit = jnp.maximum(
        row_geom[3][:, None] * delta_x
        + row_geom[4][:, None] * delta_y
        + row_geom[5][:, None] * delta_z,
        0.0,
    )
    cos_recv = jnp.maximum(
        -(
            col_geom[3][None, :] * delta_x
            + col_geom[4][None, :] * delta_y
            + col_geom[5][None, :] * delta_z
        ),
        0.0,
    )
    patch_area = row_geom[6][:, None]
    spread = dist_sq + patch_area
    kernel = cos_emit * cos_recv * patch_area / (math.pi * spread * spread)
    row_blocks, col_blocks = block_mask.shape
    rows_total = row_geom.shape[1]
    cols_total = col_geom.shape[1]
    expanded = jnp.broadcast_to(
        block_mask[:, None, :, None],
        (row_blocks, rows_total // row_blocks, col_blocks, cols_total // col_blocks),
    ).reshape(rows_total, cols_total)
    return (expanded * kernel).astype(jnp.bfloat16)


def block_width():
    return 128


def local(
    positions,
    angles,
    areas,
    emissivity,
    emission,
    radiosity_in,
    adjoint_in,
    visibility,
    inlet_patches,
    inlet_weights,
):
    emit_count = lax.axis_size("emit")
    recv_count = lax.axis_size("recv")
    emit_index = lax.axis_index("emit")
    recv_index = lax.axis_index("recv")
    own_count = areas.shape[0]
    cases = emission.shape[0]
    geometry = patch_geometry(positions, angles, areas)
    reflect = 1.0 - emissivity
    own_weights = (reflect[None, :] * adjoint_in).astype(jnp.bfloat16)
    own_values = radiosity_in.astype(jnp.bfloat16)
    mask_rows = visibility.shape[0]
    per_block = visibility.shape[1] // emit_count
    own_blocks = own_count // BLK
    folded_mask = visibility.astype(jnp.float32).reshape(mask_rows, emit_count, per_block)
    tile_mask = lax.dynamic_slice_in_dim(
        folded_mask, recv_index * own_blocks, own_blocks, 2
    ).reshape(mask_rows, emit_count * own_blocks)
    row_total = own_count * recv_count
    col_total = own_count * emit_count
    row_values = lax.all_gather(own_values, "recv", axis=1, tiled=True)
    col_weight = lax.all_gather(own_weights, "emit", axis=1, tiled=True)
    start_state = (
        jnp.zeros((cases, col_total), jnp.float32),
        jnp.zeros((cases, row_total), jnp.float32),
    )
    col_geom = lax.all_gather(geometry, "emit", axis=1, tiled=True)
    geom_piece = lax.all_gather(geometry, "recv", axis=1, tiled=True)
    count = geom_piece.shape[1]
    width = block_width()

    def inner(number, state):
        fwd_total, adj_total = state
        offset = number * width
        geom_part = lax.dynamic_slice_in_dim(geom_piece, offset, width, 1)
        value_part = lax.dynamic_slice_in_dim(row_values, offset, width, 1)
        mask_part = lax.dynamic_slice_in_dim(tile_mask, offset // BLK, width // BLK, 0)
        tile = view_tile(geom_part, col_geom, mask_part)
        fwd_total = fwd_total + jnp.dot(value_part, tile, preferred_element_type=jnp.float32)
        adj_part = lax.dot_general(
            col_weight, tile, (((1,), (1,)), ((), ())), preferred_element_type=jnp.float32
        )
        adj_total = lax.dynamic_update_slice_in_dim(adj_total, adj_part, offset, 1)
        return (fwd_total, adj_total)

    forward, adjoint = lax.fori_loop(0, count // width, inner, start_state)
    incoming = lax.psum_scatter(forward, "emit", scatter_dimension=1, tiled=True)
    returned = lax.psum_scatter(adjoint, "recv", scatter_dimension=1, tiled=True)
    own_ids = (emit_index * recv_count + recv_index) * own_count + lax.iota(jnp.int32, own_count)
    selector = (inlet_patches[:, None] == own_ids[None, :]).astype(jnp.float32)
    source = jnp.dot(
        inlet_weights, selector, precision=lax.Precision.HIGHEST, preferred_element_type=jnp.float32
    )
    radiosity_out = emissivity[None, :] * emission + reflect[None, :] * incoming
    adjoint_out = source + returned
    emissivity_grad = jnp.sum(adjoint_out * (emission - incoming), axis=0)
    return (radiosity_out, adjoint_out, emissivity_grad)


def solution(mesh):
    placed = (
        P(None, ("groups", "emit", "recv")),
        P(None, ("groups", "emit", "recv")),
        P(("groups", "emit", "recv")),
        P(("groups", "emit", "recv")),
        P(None, ("groups", "emit", "recv")),
        P(None, ("groups", "emit", "recv")),
        P(None, ("groups", "emit", "recv")),
        P(("groups", "emit"), None),
        P("groups"),
        P(None, "groups"),
    )
    return jax.shard_map(
        local,
        mesh=mesh,
        in_specs=placed,
        out_specs=(
            P(None, ("groups", "emit", "recv")),
            P(None, ("groups", "emit", "recv")),
            P(("groups", "emit", "recv")),
        ),
        check_vma=False,
    )
```

profile of v0, /device:TPU:0, one launch (start us, length us, event | category | flops | bytes accessed | tf_op | source)
XLA Modules:
  0.0 115.8 jit_solution(4974398801967030085)
XLA Ops:
  7.2 0.0 copy-start
  7.2 0.0 reduce-scatter.5.cloned.1.call-start
  7.2 0.8 slice_cosine_fusion
  8.1 0.7 concatenate.3
  8.8 14.8 %all_gather.14 = f32[7,1024]{1,0:T(8,128)S(1)} all-gather(f32[7,256]{1,0:T(8,128)S(1)} %concatenate.3), channel_id=1, replica_groups=mesh['groups'=2,'emit'=4,'recv'=4] {'emit'}, dimensions={1}, use_global_device_ids=true | all-gather | bytes 35840 | tf_op jit(solution)/shard_map/all_gather | solution.py:92
  23.6 5.2 %all_gather.13 = f32[7,1024]{1,0:T(8,128)S(1)} all-gather(f32[7,256]{1,0:T(8,128)S(1)} %concatenate.3), channel_id=1, replica_groups=mesh['groups'=2,'emit'=4,'recv'=4] {'recv'}, dimensions={1}, use_global_device_ids=true | all-gather | bytes 35840 | tf_op jit(solution)/shard_map/all_gather | solution.py:93
  28.8 0.7 broadcast_subtract_fusion
  29.5 0.7 convert_element_type.21
  30.1 0.1 copy.15
  30.2 0.1 copy.14
  30.3 0.8 convert_element_type.20
  31.1 5.2 %all_gather.12 = bf16[32,1024]{1,0:T(8,128)(2,1)S(1)} all-gather(bf16[32,256]{1,0:T(8,128)(2,1)S(1)} %convert_element_type.20), channel_id=1, replica_groups=mesh['groups'=2,'emit'=4,'recv'=4] {'recv'}, dimensions={1}, use_global_device_ids=true | all-gather | bytes 81920 | tf_op jit(solution)/shard_map/all_gather | solution.py:86
  36.3 13.1 %all_gather.15 = bf16[32,1024]{1,0:T(8,128)(2,1)S(1)} all-gather(bf16[32,256]{1,0:T(8,128)(2,1)S(1)} %multiply_convert_fusion), channel_id=1, replica_groups=mesh['groups'=2,'emit'=4,'recv'=4] {'emit'}, dimensions={1}, use_global_device_ids=true | all-gather | bytes 81920 | tf_op jit(solution)/shard_map/all_gather | solution.py:87
  49.4 13.7 %while.18 = (s32[]{:T(128)}, f32[32,1024]{1,0:T(8,128)S(1)}, f32[32,1024]{1,0:T(8,128)S(1)}, bf16[32,1024]{1,0:T(8,128)(2,1)S(1)}, f32[8,8]{1,0:T(8,128)S(1)}, /...) while((s32[]{:T(128)}, f32[32,1024]{1,0:T(8,128)S(1)}, ...), condition=%wide.region_1.2_spmd.clone, body=%wide.region_0.1_spmd.clone.sunk | while | flops 24444952 | bytes 484852 | solution.py:111
  49.5 0.1 broadcast_bitcast_fusion.2
  49.6 0.8 convolution_add_fusion.2
  50.4 0.8 fusion.47
  51.2 0.1 broadcast_bitcast_fusion.2
  51.3 0.8 convolution_add_fusion.2
  52.1 0.8 fusion.47
  52.9 0.1 broadcast_bitcast_fusion.2
  53.0 0.8 convolution_add_fusion.2
  53.8 0.8 fusion.47
  54.6 0.1 broadcast_bitcast_fusion.2
  54.7 0.8 convolution_add_fusion.2
  55.5 0.8 fusion.47
  56.3 0.1 broadcast_bitcast_fusion.2
  56.4 0.8 convolution_add_fusion.2
  57.2 0.8 fusion.47
  58.0 0.1 broadcast_bitcast_fusion.2
  58.1 0.8 convolution_add_fusion.2
  58.9 0.8 fusion.47
  59.7 0.1 broadcast_bitcast_fusion.2
  59.8 0.8 convolution_add_fusion.2
  60.6 0.8 fusion.47
  61.4 0.1 broadcast_bitcast_fusion.2
  61.5 0.8 convolution_add_fusion.2
  62.4 0.8 fusion.47
  63.1 0.0 copy-start.1
  63.2 0.0 copy-start.5
  63.2 0.0 copy-start.6
  63.2 0.6 copy-done.1
  63.8 0.0 reduce-scatter.5.cloned.1.call-update
  63.8 0.0 reduce-scatter.3.cloned.1.call-start
  63.9 0.7 reduce-scatter.3.cloned.1.call-update
  64.6 20.0 %reduce-scatter.5.cloned.1.call-done = f32[32,256]{1,0:T(8,128)} async-done(((f32[32,1024]{1,0:T(8,128)}), f32[32,256]{1,0:T(8,128)}) %reduce-scatter.5.cloned.1.call-update) | async-done | bytes 32784 | tf_op jit(solution)/shard_map/reduce_scatter | solution.py:113
  84.6 21.6 %reduce-scatter.3.cloned.1.call-done = f32[32,256]{1,0:T(8,128)} async-done(((f32[32,1024]{1,0:T(8,128)}), f32[32,256]{1,0:T(8,128)}) %reduce-scatter.3.cloned.1.call-update) | async-done | bytes 32784 | tf_op jit(solution)/shard_map/reduce_scatter | solution.py:112
  106.2 2.8 %multiply_reduce_fusion = (f32[256]{0:T(256)}, f32[32,256]{1,0:T(8,128)}, f32[32,256]{1,0:T(8,128)}) fusion(f32[32,256]{1,0:T(8,128)S(1)} %copy-done.5, f32[32,256]{1,0:T(8,128)} %reduce-scatter.3.cloned.1.call-done, f32[256]{0:T(256)S(1)} %broadcast_subtract_fusion, f32[256]{0:T(256)S(1)} %copy-done.4, f32[32,256]{1,0:T(8,128)} %reduce-scatter.5.cloned.1.call-done, ...), kind=kOutput, calls=%fused_computation.47 | convolution fusion | flops 201907968 | bytes 438272 | tf_op jit(solution)/shard_map/dot_general | solution.py:116
  (46 shorter events, 0.4 us)
Async XLA Ops:
  7.2 99.0 %copy-start = (f32[32,2048]{1,0:T(8,128)S(1)}, f32[32,2048]{1,0:T(8,128)}, u32[]{:S(2)}) copy-start(f32[32,2048]{1,0:T(8,128)} %param.21) | copy-start | bytes 786436
  7.2 29.1 %copy-start.3 = (f32[32,256]{1,0:T(8,128)S(1)}, f32[32,256]{1,0:T(8,128)}, u32[]{:S(2)}) copy-start(f32[32,256]{1,0:T(8,128)} %param.18) | copy-start | bytes 98308
  7.2 77.4 %reduce-scatter.5.cloned.1.call-start = ((), (), s32[]{:S(2)}) async-start(), calls=%async_computation.3 | async-start | bytes 163840 | tf_op jit(solution)/shard_map/reduce_scatter | solution.py:113
  63.1 0.7 copy-start.1
  63.1 0.7 copy-start.2
  63.1 43.0 %copy-start.4 = (f32[256]{0:T(256)S(1)}, f32[256]{0:T(256)}, u32[]{:S(2)}) copy-start(f32[256]{0:T(256)} %param.15) | copy-start | bytes 3076
  63.2 43.0 %copy-start.5 = (f32[32,256]{1,0:T(8,128)S(1)}, f32[32,256]{1,0:T(8,128)}, u32[]{:S(2)}) copy-start(f32[32,256]{1,0:T(8,128)} %param.16) | copy-start | bytes 98308
  63.2 43.0 %copy-start.6 = (s32[2048]{0:T(1024)S(1)}, s32[2048]{0:T(1024)}, u32[]{:S(2)}) copy-start(s32[2048]{0:T(1024)} %param.20) | copy-start | bytes 24580
  63.8 42.3 %reduce-scatter.3.cloned.1.call-start = ((), (), s32[]{:S(2)}) async-start(), calls=%async_computation.2 | async-start | bytes 163840 | tf_op jit(solution)/shard_map/reduce_scatter | solution.py:112
Sparse Core Ops, SparseCore 0:
  63.9 20.5 reduce-scatter.4
  86.9 19.1 reduce-scatter.2
where the time goes:
time: 116 us
  waiting for transfers between devices  42.3 us (36%)
  blocking collectives  38.3 us (33%)
  matrix products  15.3 us (13%)
  between operations  14.1 us (12%)
  other arithmetic  2.97 us (3%)
  local copies, waits for them, and re-layouts  2.42 us (2%)
    reduce_scatter x1, waiting for transfers between devices, local(): lax.psum_scatter(forward, 'emit', scatter_dimension=1, tiled=True)  21.6 us
    reduce_scatter x1, waiting for transfers between devices, local(): lax.psum_scatter(adjoint, 'recv', scatter_dimension=1, tiled=True)  20 us
    all_gather x1, blocking collectives, local(): col_geom = lax.all_gather(geometry, 'emit', axis=1, tiled=True)  14.8 us
    all_gather x1, blocking collectives, local(): col_weight = lax.all_gather(own_weights, 'emit', axis=1, tiled=True)  13.1 us
    dot_general x8, matrix products, inner(): jnp.dot(value_part, tile, preferred_element_type=jnp.float32)  6.43 us
    dot_general x8, matrix products, inner(): lax.dot_general(col_weight, tile, (((1,), (1,)), ((), ())), preferred_ele...  6.15 us
    all_gather x1, blocking collectives, local(): row_values = lax.all_gather(own_values, 'recv', axis=1, tiled=True)  5.23 us
    all_gather x1, blocking collectives, local(): geom_piece = lax.all_gather(geometry, 'recv', axis=1, tiled=True)  5.18 us
  transfers between devices with their start and end apart: 2, of which 2 were waited for; matrix products, arithmetic and copies ran while one was open for 0% of the time, Pallas kernels for 0%

commit v1 on v0

--- a/solution.py
+++ b/solution.py
@@ -84,7 +84,12 @@
     row_total = own_count * recv_count
     col_total = own_count * emit_count
     row_values = lax.all_gather(own_values, "recv", axis=1, tiled=True)
-    col_weight = lax.all_gather(own_weights, "emit", axis=1, tiled=True)
+    ring = [own_weights]
+    for hop in range(3):
+        ring.append(lax.ppermute(ring[-1], "emit", [(dev, (dev + 1) % 4) for dev in range(4)]))
+    col_weight = jnp.roll(
+        jnp.concatenate(ring[::-1], axis=1), (lax.axis_index("emit") + 1) * ring[0].shape[1], axis=1
+    )
     start_state = (
         jnp.zeros((cases, col_total), jnp.float32),
         jnp.zeros((cases, row_total), jnp.float32),

time: 116 us -> 107 us (0.922)
  blocking collectives: 38.3 us -> 23.5 us
  starting transfers between devices: 0.08 us -> 5.77 us
    all_gather x1 -> x0, blocking collectives: 13.1 us -> none  [local(): col_weight = lax.all_gather(own_weights, 'emit', axis=1, tiled=True)]
    ppermute x0 -> x3, starting transfers between devices: none -> 5.69 us  [local(): lax.ppermute(ring[-1], 'emit', [(dev, (dev + 1) % 4) for dev in range(4)])]
    all_gather x1, blocking collectives: 14.8 us -> 13.1 us  [local(): col_geom = lax.all_gather(geometry, 'emit', axis=1, tiled=True)]
  transfers between devices with their start and end apart: 2 -> 5, of which waited for: 2 -> 3; matrix products, arithmetic and copies ran while one was open for 0% -> 3% of each run, Pallas kernels for 0% -> 0%
where the time goes in v1:
time: 107 us
  waiting for transfers between devices  41.7 us (39%)
  blocking collectives  23.5 us (22%)
  matrix products  15.3 us (14%)
  between operations  14.2 us (13%)
  starting transfers between devices  5.77 us (5%)
  other arithmetic  3.75 us (4%)
  local copies, waits for them, and re-layouts  2.46 us (2%)
    reduce_scatter x1, waiting for transfers between devices, local(): lax.psum_scatter(forward, 'emit', scatter_dimension=1, tiled=True)  21.6 us
    reduce_scatter x1, waiting for transfers between devices, local(): lax.psum_scatter(adjoint, 'recv', scatter_dimension=1, tiled=True)  18.9 us
    all_gather x1, blocking collectives, local(): col_geom = lax.all_gather(geometry, 'emit', axis=1, tiled=True)  13.1 us
    dot_general x8, matrix products, inner(): jnp.dot(value_part, tile, preferred_element_type=jnp.float32)  6.43 us
    dot_general x8, matrix products, inner(): lax.dot_general(col_weight, tile, (((1,), (1,)), ((), ())), preferred_ele...  6.12 us
    ppermute x3, starting transfers between devices, local(): lax.ppermute(ring[-1], 'emit', [(dev, (dev + 1) % 4) for dev in range(4)])  5.69 us
    all_gather x1, blocking collectives, local(): row_values = lax.all_gather(own_values, 'recv', axis=1, tiled=True)  5.23 us
    all_gather x1, blocking collectives, local(): geom_piece = lax.all_gather(geometry, 'recv', axis=1, tiled=True)  5.18 us
  transfers between devices with their start and end apart: 5, of which 3 were waited for; matrix products, arithmetic and copies ran while one was open for 3% of the time, Pallas kernels for 0%

profile of v1, /device:TPU:0, one launch (start us, length us, event | category | flops | bytes accessed | tf_op | source)
XLA Modules:
  0.0 107.0 jit_solution(9925803407056718422)
XLA Ops:
  7.2 0.0 reduce-scatter.5.cloned.1.call-start
  7.2 0.7 broadcast_subtract_fusion
  7.9 0.8 multiply_convert_fusion
  8.7 3.0 %collective-permute-start = (bf16[32,256]{1,0:T(8,128)(2,1)S(1)}, bf16[32,256]{1,0:T(8,128)(2,1)S(1)}, u32[]{:S(2)}, u32[]{:S(2)}) collective-permute-start(bf16[32,256]{1,0:T(8,128)(2,1)S(1)} %multiply_convert_fusion), channel_id=1, source_target_pairs={{0,4},{4,8},{8,12},{12,0},{1,5},{5,9},{9,13},{13,1},{2,6},{6,10},{... | collective-permute-start | bytes 49160 | tf_op jit(solution)/shard_map/ppermute | solution.py:89
  11.7 0.8 slice_cosine_fusion
  12.5 0.7 convert_element_type.21
  13.2 0.1 copy.15
  13.4 0.1 copy.14
  13.4 0.8 convert_element_type.20
  14.2 0.7 concatenate.9
  14.9 0.5 collective-permute-done
  15.4 1.1 %collective-permute-start.1 = (bf16[32,256]{1,0:T(8,128)(2,1)S(1)}, bf16[32,256]{1,0:T(8,128)(2,1)S(1)}, u32[]{:S(2)}, u32[]{:S(2)}) collective-permute-start(bf16[32,256]{1,0:T(8,128)(2,1)S(1)} %collective-permute-done), channel_id=1, source_target_pairs={{0,4},{4,8},{8,12},{12,0},{1,5},{5,9},{9,13},{13,1},{2,6},{6,10},{... | collective-permute-start | bytes 49160 | tf_op jit(solution)/shard_map/ppermute | solution.py:89
  16.5 5.2 %all_gather.9 = bf16[32,1024]{1,0:T(8,128)(2,1)S(1)} all-gather(bf16[32,256]{1,0:T(8,128)(2,1)S(1)} %convert_element_type.20), channel_id=1, replica_groups=mesh['groups'=2,'emit'=4,'recv'=4] {'recv'}, dimensions={1}, use_global_device_ids=true | all-gather | bytes 81920 | tf_op jit(solution)/shard_map/all_gather | solution.py:86
  21.8 1.6 %collective-permute-start.2 = (bf16[32,256]{1,0:T(8,128)(2,1)S(1)}, bf16[32,256]{1,0:T(8,128)(2,1)S(1)}, u32[]{:S(2)}, u32[]{:S(2)}) collective-permute-start(bf16[32,256]{1,0:T(8,128)(2,1)S(1)} %collective-permute-done.1), channel_id=1, source_target_pairs={{0,4},{4,8},{8,12},{12,0},{1,5},{5,9},{9,13},{13,1},{2,6},{6,10},{... | collective-permute-start | bytes 49160 | tf_op jit(solution)/shard_map/ppermute | solution.py:89
  23.3 13.1 %all_gather.11 = f32[7,1024]{1,0:T(8,128)S(1)} all-gather(f32[7,256]{1,0:T(8,128)S(1)} %concatenate.9), channel_id=1, replica_groups=mesh['groups'=2,'emit'=4,'recv'=4] {'emit'}, dimensions={1}, use_global_device_ids=true | all-gather | bytes 35840 | tf_op jit(solution)/shard_map/all_gather | solution.py:97
  36.5 5.2 %all_gather.10 = f32[7,1024]{1,0:T(8,128)S(1)} all-gather(f32[7,256]{1,0:T(8,128)S(1)} %concatenate.9), channel_id=1, replica_groups=mesh['groups'=2,'emit'=4,'recv'=4] {'recv'}, dimensions={1}, use_global_device_ids=true | all-gather | bytes 35840 | tf_op jit(solution)/shard_map/all_gather | solution.py:98
  41.8 13.7 %while.18 = (s32[]{:T(128)}, f32[32,1024]{1,0:T(8,128)S(1)}, f32[32,1024]{1,0:T(8,128)S(1)}, bf16[32,1024]{1,0:T(8,128)(2,1)S(1)}, f32[8,8]{1,0:T(8,128)S(1)}, /...) while((s32[]{:T(128)}, f32[32,1024]{1,0:T(8,128)S(1)}, ...), condition=%wide.region_1.2_spmd.clone, body=%wide.region_0.1_spmd.clone.sunk | while | flops 24444952 | bytes 484852 | solution.py:116
  41.8 0.1 broadcast_bitcast_fusion.2
  41.9 0.8 convolution_add_fusion.2
  42.7 0.8 fusion.47
  43.5 0.1 broadcast_bitcast_fusion.2
  43.6 0.8 convolution_add_fusion.2
  44.5 0.8 fusion.47
  45.2 0.1 broadcast_bitcast_fusion.2
  45.3 0.8 convolution_add_fusion.2
  46.2 0.8 fusion.47
  46.9 0.1 broadcast_bitcast_fusion.2
  47.1 0.8 convolution_add_fusion.2
  47.9 0.8 fusion.47
  48.7 0.1 broadcast_bitcast_fusion.2
  48.8 0.8 convolution_add_fusion.2
  49.6 0.8 fusion.47
  50.4 0.1 broadcast_bitcast_fusion.2
  50.5 0.8 convolution_add_fusion.2
  51.3 0.8 fusion.47
  52.1 0.1 broadcast_bitcast_fusion.2
  52.2 0.8 convolution_add_fusion.2
  53.0 0.8 fusion.47
  53.8 0.1 broadcast_bitcast_fusion.2
  53.9 0.8 convolution_add_fusion.2
  54.7 0.8 fusion.47
  55.5 0.6 copy-done.1
  56.1 0.0 reduce-scatter.5.cloned.1.call-update
  56.1 0.0 reduce-scatter.3.cloned.1.call-start
  56.2 0.7 reduce-scatter.3.cloned.1.call-update
  56.9 18.9 %reduce-scatter.5.cloned.1.call-done = f32[32,256]{1,0:T(8,128)} async-done(((f32[32,1024]{1,0:T(8,128)}), f32[32,256]{1,0:T(8,128)}) %reduce-scatter.5.cloned.1.call-update) | async-done | bytes 32784 | tf_op jit(solution)/shard_map/reduce_scatter | solution.py:118
  75.8 21.6 %reduce-scatter.3.cloned.1.call-done = f32[32,256]{1,0:T(8,128)} async-done(((f32[32,1024]{1,0:T(8,128)}), f32[32,256]{1,0:T(8,128)}) %reduce-scatter.3.cloned.1.call-update) | async-done | bytes 32784 | tf_op jit(solution)/shard_map/reduce_scatter | solution.py:117
  97.4 2.8 %multiply_reduce_fusion = (f32[256]{0:T(256)}, f32[32,256]{1,0:T(8,128)}, f32[32,256]{1,0:T(8,128)}) fusion(f32[32,256]{1,0:T(8,128)S(1)} %copy-done.5, f32[32,256]{1,0:T(8,128)} %reduce-scatter.3.cloned.1.call-done, f32[256]{0:T(256)S(1)} %broadcast_subtract_fusion, f32[256]{0:T(256)S(1)} %copy-done.4, f32[32,256]{1,0:T(8,128)} %reduce-scatter.5.cloned.1.call-done, ...), kind=kOutput, calls=%fused_computation.47 | convolution fusion | flops 201907968 | bytes 438272 | tf_op jit(solution)/shard_map/dot_general | solution.py:121
  (60 shorter events, 0.5 us)
Async XLA Ops:
  7.2 90.2 %copy-start = (f32[32,2048]{1,0:T(8,128)S(1)}, f32[32,2048]{1,0:T(8,128)}, u32[]{:S(2)}) copy-start(f32[32,2048]{1,0:T(8,128)} %param.21) | copy-start | bytes 786436
  7.2 34.5 %copy-start.2 = (f32[32,256]{1,0:T(8,128)S(1)}, f32[32,256]{1,0:T(8,128)}, u32[]{:S(2)}) copy-start(f32[32,256]{1,0:T(8,128)} %param.18) | copy-start | bytes 98308
  7.2 68.6 %reduce-scatter.5.cloned.1.call-start = ((), (), s32[]{:S(2)}) async-start(), calls=%async_computation.3 | async-start | bytes 163840 | tf_op jit(solution)/shard_map/reduce_scatter | solution.py:118
  8.7 6.8 %collective-permute-start = (bf16[32,256]{1,0:T(8,128)(2,1)S(1)}, bf16[32,256]{1,0:T(8,128)(2,1)S(1)}, u32[]{:S(2)}, u32[]{:S(2)}) collective-permute-start(bf16[32,256]{1,0:T(8,128)(2,1)S(1)} %multiply_convert_fusion), channel_id=1, source_target_pairs={{0,4},{4,8},{8,12},{12,0},{1,5},{5,9},{9,13},{13,1},{2,6},{6,10},{... | collective-permute-start | bytes 49160 | tf_op jit(solution)/shard_map/ppermute | solution.py:89
  15.4 6.3 %collective-permute-start.1 = (bf16[32,256]{1,0:T(8,128)(2,1)S(1)}, bf16[32,256]{1,0:T(8,128)(2,1)S(1)}, u32[]{:S(2)}, u32[]{:S(2)}) collective-permute-start(bf16[32,256]{1,0:T(8,128)(2,1)S(1)} %collective-permute-done), channel_id=1, source_target_pairs={{0,4},{4,8},{8,12},{12,0},{1,5},{5,9},{9,13},{13,1},{2,6},{6,10},{... | collective-permute-start | bytes 49160 | tf_op jit(solution)/shard_map/ppermute | solution.py:89
  21.8 19.9 %collective-permute-start.2 = (bf16[32,256]{1,0:T(8,128)(2,1)S(1)}, bf16[32,256]{1,0:T(8,128)(2,1)S(1)}, u32[]{:S(2)}, u32[]{:S(2)}) collective-permute-start(bf16[32,256]{1,0:T(8,128)(2,1)S(1)} %collective-permute-done.1), channel_id=1, source_target_pairs={{0,4},{4,8},{8,12},{12,0},{1,5},{5,9},{9,13},{13,1},{2,6},{6,10},{... | collective-permute-start | bytes 49160 | tf_op jit(solution)/shard_map/ppermute | solution.py:89
  55.4 0.7 copy-start.1
  55.5 0.7 copy-start.3
  55.5 41.9 %copy-start.4 = (f32[256]{0:T(256)S(1)}, f32[256]{0:T(256)}, u32[]{:S(2)}) copy-start(f32[256]{0:T(256)} %param.15) | copy-start | bytes 3076
  55.5 41.9 %copy-start.5 = (f32[32,256]{1,0:T(8,128)S(1)}, f32[32,256]{1,0:T(8,128)}, u32[]{:S(2)}) copy-start(f32[32,256]{1,0:T(8,128)} %param.16) | copy-start | bytes 98308
  55.5 41.8 %copy-start.6 = (s32[2048]{0:T(1024)S(1)}, s32[2048]{0:T(1024)}, u32[]{:S(2)}) copy-start(s32[2048]{0:T(1024)} %param.20) | copy-start | bytes 24580
  56.1 41.2 %reduce-scatter.3.cloned.1.call-start = ((), (), s32[]{:S(2)}) async-start(), calls=%async_computation.2 | async-start | bytes 163840 | tf_op jit(solution)/shard_map/reduce_scatter | solution.py:117
Sparse Core Ops, SparseCore 0:
  56.3 19.4 reduce-scatter.4
  78.1 19.1 reduce-scatter.2
